TPU v7x, 256 devices: a whole 4x4x8 slice. The times are simulated.
256 devices in a mesh: role: 2 (over core), grp: 4 (over x), seq: 32 (over z, y).
Axes of the slice: x: 4, y: 4, z: 8, core: 2. Of those that a mesh axis runs over, the one named last changes fastest.
Arguments:
- tokens: bfloat16 [8, 2048, 2048], P(('role', 'grp'), 'seq'), may hold values from -8 to 8
- parents: int32 [8, 64], P(('role', 'grp')), may hold values from 0 to 62, as said below
- route_ids: int32 [8, 2048, 8], P(('role', 'grp'), 'seq'), may hold values from 0 to 127, all different within a row; in each aligned block of 64 rows (0 to 63, 64 to 127, ..., all dimensions but the last counted through in order) at most 6 rows name the same one
- route_gates: float32 [8, 2048, 8], P(('role', 'grp'), 'seq'), may hold values from 0.02 to 0.25
- input_gain: float32 [2048], replicated, may hold values from 0.1 to 1.9
- q_gain: float32 [128], replicated, may hold values from 0.5 to 25
- k_gain: float32 [128], replicated, may hold values from 0.5 to 25
- post_gain: float32 [2048], replicated, may hold values from 0.1 to 1.9
- w_query: bfloat16 [2048, 4096], P(None, 'seq'), may hold values from -0.125 to 0.125
- w_keyval: bfloat16 [4, 2048, 256], replicated, may hold values from -0.125 to 0.125
- w_out: bfloat16 [4096, 2048], P('seq'), may hold values from -0.09375 to 0.09375
- w_gate_up: bfloat16 [128, 2, 2048, 768], P(('grp', 'seq'), None, None, 'role'), may hold values from -0.125 to 0.125
- w_down: bfloat16 [128, 768, 2048], P(('grp', 'seq'), 'role'), may hold values from -0.21875 to 0.21875
Outputs:
- layer_out: bfloat16 [8, 2048, 2048], P(('role', 'grp'), 'seq')
Inputs may be any that keep to these rules, and one draw needn't show every extreme that they name: parents[s, 0] = 0; for a >= 1, parents[s, a] < a; the last node's parent is node 62. `route_ids`: each token names 8 different experts; among the 64 tokens of one device no expert is named more than 6 times, and in every draw some expert is named exactly 6 times by the tokens of some device.
All inputs are finite; a program needn't handle non-finite values.
Results may differ from a plain program's by a relative error of at most 0.018.
The roundings to bfloat16 on the way count: a program that leaves them out, or rounds other values in their place, can miss the bound.
Values may be sent and summed in bfloat16 or wider, within the bound.
No kernel may reach another device: no remote copies, remote signals or barrier semaphores. Data moves between devices by JAX's collectives and lax.ppermute only.
A program may use at most 128 MiB of HBM per device.

v0:
```python
import math
import jax
import jax.numpy as jnp
from jax import lax
from jax.sharding import PartitionSpec as P

NODE = 32
EPSILON = 1e-06
ROPE_BASE = 1000000.0
HIGHEST = lax.Precision.HIGHEST
MASKED = -1e30


def turned_gather(arrays, axis, dims):
    turned = [jnp.moveaxis(a, dim, 0) for a, dim in zip(arrays, dims)]
    both = jnp.concatenate([t.reshape(len(t), -1) for t in turned], axis=1)
    result, at, gathered = (lax.all_gather(both, axis, axis=0, tiled=True), 0, [])
    for t, dim in zip(turned, dims):
        slab = result[:, at : at + t[0].size].reshape(-1, *t.shape[1:])
        gathered.append(jnp.moveaxis(slab, 0, dim))
        at += t[0].size
    return tuple(gathered)


def rms_scale(values, gain):
    mean_sq = jnp.mean(values * values, axis=-1, keepdims=True)
    return values * lax.rsqrt(mean_sq + EPSILON) * gain


def ancestry(parent_row, node_count):
    node_ids = jnp.arange(node_count, dtype=jnp.int32)
    parent_hot = (parent_row[:, None] == node_ids[None, :]).astype(jnp.float32)
    reach_table = jnp.maximum(parent_hot, jnp.eye(node_count, dtype=jnp.float32))
    for repeat_index in range(node_count.bit_length()):
        reach_table = (jnp.dot(reach_table, reach_table, precision=HIGHEST) > 0.5).astype(
            jnp.float32
        )
    return reach_table


def token_positions(parent_row, length):
    reach_table = ancestry(parent_row, length // NODE)
    depth = jnp.sum(reach_table, axis=1) - 1.0
    offsets = (jnp.arange(length, dtype=jnp.int32) % NODE).astype(jnp.float32)
    return (reach_table, jnp.repeat(depth, NODE) * NODE + offsets)


def rotate(values, positions):
    half_dim = values.shape[-1] // 2
    frequency = jnp.power(
        ROPE_BASE, -2.0 * jnp.arange(half_dim, dtype=jnp.float32) / values.shape[-1]
    )
    angles = positions[:, None] * frequency[None, :]
    cosine = jnp.cos(angles)[:, None, :]
    sines = jnp.sin(angles)[:, None, :]
    first_half = values[..., :half_dim]
    second = values[..., half_dim:]
    return jnp.concatenate(
        [first_half * cosine - second * sines, second * cosine + first_half * sines], axis=-1
    )


def expert_ffn(inputs, gate_up, down_proj):
    gate_proj = jnp.dot(inputs, gate_up[0], preferred_element_type=jnp.float32)
    up_proj = jnp.dot(inputs, gate_up[1], preferred_element_type=jnp.float32)
    hidden = (jax.nn.silu(gate_proj) * up_proj).astype(jnp.bfloat16)
    return jnp.dot(hidden, down_proj, preferred_element_type=jnp.float32)


def body(
    tokens,
    parents,
    route_ids,
    route_gates,
    input_gain,
    q_gain,
    k_gain,
    post_gain,
    w_query,
    w_keyval,
    w_out,
    w_gate_up,
    w_down,
):
    seq_count = lax.axis_size("seq")
    grp_count = lax.axis_size("grp")
    tok_rows = tokens.shape[1]
    model_width = tokens.shape[2]
    head_dim = q_gain.shape[0]
    local_heads = w_query.shape[1] // head_dim
    kv_count = w_keyval.shape[0]
    heads_per_kv = local_heads * seq_count // kv_count
    length = tok_rows * seq_count
    q_width = local_heads * head_dim
    residual = tokens[0].astype(jnp.float32)
    normed = rms_scale(residual, input_gain).astype(jnp.bfloat16)
    kv_index = lax.axis_index("seq") * local_heads // heads_per_kv
    keyval_weight = lax.dynamic_index_in_dim(w_keyval, kv_index, 0, keepdims=False)
    joint_weight = jnp.concatenate([w_query, keyval_weight], axis=1)
    projected = jnp.dot(
        lax.all_gather(normed, "seq", axis=0, tiled=True),
        joint_weight,
        preferred_element_type=jnp.float32,
    ).astype(jnp.bfloat16)
    reach_table, positions = token_positions(parents[0], length)
    queries = projected[:, :q_width].astype(jnp.float32).reshape(length, local_heads, head_dim)
    q_rot = rotate(rms_scale(queries, q_gain), positions).astype(jnp.bfloat16)
    keys_in = (
        projected[:, q_width : q_width + head_dim].astype(jnp.float32).reshape(length, 1, head_dim)
    )
    k_rot = rotate(rms_scale(keys_in, k_gain), positions)[:, 0].astype(jnp.bfloat16)
    values_in = projected[:, q_width + head_dim :]
    reach_rows = jnp.repeat(reach_table, NODE, axis=0)
    block_rows = min(length, 512)
    key_pos = jnp.arange(length, dtype=jnp.int32)
    inv_scale = 1.0 / math.sqrt(head_dim)

    def attend(row_start):
        q_block = lax.dynamic_slice_in_dim(q_rot, row_start, block_rows, 0)
        scores = (
            jnp.einsum("bhd,kd->hbk", q_block, k_rot, preferred_element_type=jnp.float32)
            * inv_scale
        )
        ancestors = (
            jnp.repeat(lax.dynamic_slice_in_dim(reach_rows, row_start, block_rows, 0), NODE, axis=1)
            > 0.5
        )
        query_pos = row_start + jnp.arange(block_rows, dtype=jnp.int32)
        seen = ancestors & (key_pos[None, :] <= query_pos[:, None])
        scores = jnp.where(seen[None], scores, MASKED)
        row_max = jnp.max(scores, axis=-1, keepdims=True)
        exp_scores = jnp.exp(scores - row_max)
        probs = (exp_scores / jnp.sum(exp_scores, axis=-1, keepdims=True)).astype(jnp.bfloat16)
        mixed_out = jnp.einsum("hbk,kd->bhd", probs, values_in, preferred_element_type=jnp.float32)
        return mixed_out.astype(jnp.bfloat16).reshape(block_rows, q_width)

    starts = jnp.arange(length // block_rows, dtype=jnp.int32) * block_rows
    attended = lax.map(attend, starts).reshape(length, q_width)
    token_heads = lax.all_to_all(attended, "seq", split_axis=0, concat_axis=1, tiled=True)
    attn_out = jnp.dot(
        token_heads,
        lax.all_gather(w_out, "seq", axis=0, tiled=True),
        preferred_element_type=jnp.float32,
    )
    middle = lax.optimization_barrier((residual + attn_out).astype(jnp.bfloat16))
    middle_f = middle.astype(jnp.float32)
    post_normed = rms_scale(middle_f, post_gain).astype(jnp.bfloat16)
    expert_count = grp_count * seq_count
    topk = route_ids.shape[2]
    capacity = max(4, 3 * tok_rows * topk // (2 * expert_count))
    expert_ids = route_ids[0].reshape(-1)
    expert_hot = (expert_ids[:, None] == jnp.arange(expert_count, dtype=jnp.int32)[None, :]).astype(
        jnp.int32
    )
    earlier = jnp.cumsum(expert_hot, axis=0) - expert_hot
    slot_index = jnp.sum(earlier * expert_hot, axis=1)
    target = expert_ids * capacity + slot_index
    slot_hot = (
        target[:, None] == jnp.arange(expert_count * capacity, dtype=jnp.int32)[None, :]
    ).astype(jnp.bfloat16)
    placement = jnp.sum(slot_hot.reshape(tok_rows, topk, expert_count * capacity), axis=1)
    outgoing = lax.dot_general(
        placement, post_normed, (((0,), (0,)), ((), ())), preferred_element_type=jnp.float32
    )
    outgoing = outgoing.astype(jnp.bfloat16).reshape(expert_count, capacity, model_width)
    full_gate_up, full_down = turned_gather((w_gate_up[0], w_down[0]), "role", (2, 0))
    received = lax.all_to_all(outgoing, ("grp", "seq"), split_axis=0, concat_axis=0, tiled=True)
    flat_rows = received.reshape(-1, model_width)
    returned = lax.all_to_all(
        expert_ffn(flat_rows, full_gate_up, full_down).astype(jnp.bfloat16).reshape(received.shape),
        ("grp", "seq"),
        split_axis=0,
        concat_axis=0,
        tiled=True,
    )
    returned_flat = returned.reshape(expert_count * capacity, model_width)
    picked = jnp.take(returned_flat, target, axis=0).reshape(tok_rows, topk, model_width)
    moe_sum = jnp.sum(route_gates[0][:, :, None] * picked.astype(jnp.float32), axis=1)
    return (middle_f + moe_sum).astype(jnp.bfloat16).reshape(1, tok_rows, model_width)


def solution(mesh):
    in_specs = (
        P(("role", "grp"), "seq", None),
        P(("role", "grp"), None),
        P(("role", "grp"), "seq", None),
        P(("role", "grp"), "seq", None),
        P(),
        P(),
        P(),
        P(),
        P(None, "seq"),
        P(),
        P("seq", None),
        P(("grp", "seq"), None, None, "role"),
        P(("grp", "seq"), "role", None),
    )
    out_specs = P(("role", "grp"), "seq", None)
    return jax.shard_map(body, mesh=mesh, in_specs=in_specs, out_specs=out_specs, check_vma=False)
```

profile of v0, /device:TPU:32, one launch (start us, length us, event | category | flops | bytes accessed | tf_op | source)
XLA Modules:
  0.0 528.8 jit_solution(12781115510658289095)
XLA Ops:
  6.5 1.1 fusion.54
  7.7 1.8 fusion.56
  9.5 0.7 all-gather.6.cloned.1.call-update
  10.3 1.9 copy.91
  12.2 4.5 pad_maximum_fusion
  19.4 1.3 dynamic-slice_bitcast_fusion
  20.7 88.1 %all-gather.4.cloned.1.call-done = bf16[2048,2048]{1,0:T(8,128)(2,1)} async-done(((bf16[64,2048]{1,0:T(8,128)(2,1)}), bf16[2048,2048]{1,0:T(8,128)(2,1)}) %all-gather.4.cloned.1.call-update) | async-done | bytes 8388624 | tf_op jit(solution)/shard_map/all_gather | solution.py:101
  108.9 6.8 %convolution_convert_fusion.2 = bf16[2048,384]{0,1:T(8,128)(2,1)S(1)} fusion(bf16[2048,2048]{1,0:T(8,128)(2,1)} %all-gather.4.cloned.1.call-done, bf16[2048,256]{1,0:T(8,128)(2,1)S(1)} %dynamic-slice_bitcast_fusion, bf16[2048,128]{1,0:T(8,128)(2,1)S(1)} %copy-done.6), kind=kOutput, calls=%fused_computation.27 | convolution fusion | flops 3225157632 | bytes 11534336 | tf_op jit(solution)/shard_map/dot_general | solution.py:100
  116.3 2.4 fusion.47
  119.4 35.4 %while.11 = (s32[]{:T(128)}, bf16[4,512,128]{2,1,0:T(8,128)(2,1)}, s32[4]{0:T(128)S(1)}, f32[2048,64]{0,1:T(8,128)S(1)}, bf16[2048,1,128]{0,2,1:T(8,128)(2,1)S(1...) while((s32[]{:T(128)}, bf16[4,512,128]{2,1,0:T(8,128)(2,1)}, ...), condition=%wide.region_7.8_spmd.clone, body=%wide.region_4.7_spmd.clone.sunk | while | flops 547454464 | bytes 18299552 | solution.py:138
  122.3 1.2 copy.101
  123.5 0.7 iota_add_fusion.2
  124.2 1.9 fusion.110
  126.0 0.7 fusion.111
  126.7 1.5 fusion.112
  131.2 1.2 copy.101
  132.4 0.7 iota_add_fusion.2
  133.0 1.8 fusion.110
  134.9 0.7 fusion.111
  135.6 1.5 fusion.112
  140.0 1.2 copy.101
  141.8 1.8 fusion.110
  143.7 0.7 fusion.111
  144.4 1.5 fusion.112
  148.9 1.2 copy.101
  150.7 1.8 fusion.110
  152.5 0.7 fusion.111
  153.2 1.5 fusion.112
  154.8 7.6 %all-to-all-start = ((bf16[32,64,128]{2,1,0:T(8,128)(2,1)}), bf16[32,64,128]{2,1,0:T(8,128)(2,1)S(1)}, u32[]{:S(2)}, u32[]{:S(2)}) async-start(bf16[32,64,128]{2,1,0:T(8,128)(2,1)} %bitcast.8), calls=%async_computation | async-start | bytes 1048576 | tf_op jit(solution)/shard_map/all_to_all | solution.py:139
  163.8 19.8 %all-to-all-done = bf16[32,64,128]{2,1,0:T(8,128)(2,1)S(1)} async-done(((bf16[32,64,128]{2,1,0:T(8,128)(2,1)}), bf16[32,64,128]{2,1,0:T(8,128)(2,1)S(1)}, u32[]{:S(2)}, u32[]{:S(2)}) %all-to-all-start) | async-done | bytes 524320 | tf_op jit(solution)/shard_map/all_to_all | solution.py:139
  183.6 70.4 %all-gather.6.cloned.1.call-done = bf16[4096,2048]{1,0:T(8,128)(2,1)} async-done(((bf16[128,2048]{1,0:T(8,128)(2,1)}), bf16[4096,2048]{1,0:T(8,128)(2,1)}) %all-gather.6.cloned.1.call-update) | async-done | bytes 16777232 | tf_op jit(solution)/shard_map/all_gather | solution.py:142
  254.0 8.8 %fusion.21 = bf16[64,2048]{1,0:T(8,128)(2,1)S(1)} fusion(bf16[4096,2048]{1,0:T(8,128)(2,1)} %all-gather.6.cloned.1.call-done, bf16[1,64,2048]{2,1,0:T(8,128)(2,1)S(1)} %copy-done, bf16[32,64,128]{2,1,0:T(8,128)(2,1)S(1)} %all-to-all-done), kind=kOutput, calls=%fused_computation.30 | convolution fusion | flops 1074135040 | bytes 17825792 | tf_op jit(solution)/shard_map/dot_general | solution.py:140
  262.9 1.0 convolution_convert_fusion.1
  264.0 2.8 reshape.391
  266.8 13.0 %all-to-all-start.1 = ((bf16[128,6,2048]{2,1,0:T(8,128)(2,1)}), bf16[128,6,2048]{2,1,0:T(8,128)(2,1)}, u32[]{:S(2)}, u32[]{:S(2)}) async-start(bf16[128,6,2048]{2,1,0:T(8,128)(2,1)} %reshape.391), calls=%async_computation.1 | async-start | bytes 8388608 | tf_op jit(solution)/shard_map/all_to_all | solution.py:167
  279.8 3.1 all-gather.8.cloned.1.call-done
  282.9 5.8 %slice.62 = bf16[768,4096]{0,1:T(8,128)(2,1)} slice(bf16[768,6144]{0,1:T(8,128)(2,1)} %all-gather.8.cloned.1.call-done), slice={[0:768], [0:4096]} | slice | bytes 12582912 | tf_op jit(solution)/shard_map/slice | solution.py:19
  288.7 88.1 %all-to-all-done.1 = bf16[128,6,2048]{2,1,0:T(8,128)(2,1)} async-done(((bf16[128,6,2048]{2,1,0:T(8,128)(2,1)}), bf16[128,6,2048]{2,1,0:T(8,128)(2,1)}, u32[]{:S(2)}, u32[]{:S(2)}) %all-to-all-start.1) | async-done | bytes 3145760 | tf_op jit(solution)/shard_map/all_to_all | solution.py:167
  376.9 4.9 reshape.392
  381.7 5.9 %fusion.20 = f32[768,768]{1,0:T(8,128)} fusion(bf16[768,2048]{1,0:T(8,128)(2,1)S(1)} %reshape.392, bf16[2,2048,768]{2,1,0:T(8,128)(2,1)} %bitcast.135), kind=kOutput, calls=%fused_computation.26 | convolution fusion | flops 2415919104 | bytes 8650752 | tf_op jit(solution)/shard_map/dot_general | solution.py:64
  387.6 11.0 %convolution_convert_fusion = bf16[768,2048]{1,0:T(8,128)(2,1)} fusion(bf16[768,6144]{0,1:T(8,128)(2,1)} %all-gather.8.cloned.1.call-done, f32[768,768]{1,0:T(8,128)} %fusion.20, bf16[768,2048]{1,0:T(8,128)(2,1)S(1)} %reshape.392, bf16[2,2048,768]{2,1,0:T(8,128)(2,1)} %bitcast.136), kind=kOutput, calls=%fused_computation.20 | convolution fusion | flops 4836950016 | bytes 14942208 | tf_op jit(solution)/shard_map/dot_general | solution.py:67
  398.6 6.3 %reshape.395 = bf16[128,6,2048]{2,1,0:T(8,128)(2,1)} reshape(bf16[768,2048]{1,0:T(8,128)(2,1)} %convolution_convert_fusion) | data formatting | bytes 6291456 | tf_op jit(solution)/shard_map/reshape | solution.py:170
  404.9 7.9 %all-to-all-start.2 = ((bf16[128,6,2048]{2,1,0:T(8,128)(2,1)}), bf16[128,6,2048]{2,1,0:T(8,128)(2,1)}, u32[]{:S(2)}, u32[]{:S(2)}) async-start(bf16[128,6,2048]{2,1,0:T(8,128)(2,1)} %reshape.395), calls=%async_computation.2 | async-start | bytes 8388608 | tf_op jit(solution)/shard_map/all_to_all | solution.py:169
  413.2 96.1 %all-to-all-done.2 = bf16[128,6,2048]{2,1,0:T(8,128)(2,1)} async-done(((bf16[128,6,2048]{2,1,0:T(8,128)(2,1)}), bf16[128,6,2048]{2,1,0:T(8,128)(2,1)}, u32[]{:S(2)}, u32[]{:S(2)}) %all-to-all-start.2) | async-done | bytes 3145760 | tf_op jit(solution)/shard_map/all_to_all | solution.py:169
  509.3 4.9 reshape.396
  514.2 3.3 gather_fusion
  517.5 4.0 multiply_reduce_fusion
  521.5 0.8 fusion.59
  (86 shorter events, 11.0 us)
Async XLA Ops:
  6.5 102.3 %all-gather.4.cloned.1.call-start = ((), (), s32[]{:S(2)}) async-start(), calls=%async_computation.3 | async-start | bytes 8650752 | tf_op jit(solution)/shard_map/all_gather | solution.py:101
  9.5 244.5 %all-gather.6.cloned.1.call-start = ((), (), s32[]{:S(2)}) async-start(), calls=%async_computation.4 | async-start | bytes 17301504 | tf_op jit(solution)/shard_map/all_gather | solution.py:142
  10.2 272.7 %all-gather.8.cloned.1.call-start = ((), (), s32[]{:S(2)}) async-start(), calls=%async_computation.5 | async-start | bytes 14155776 | tf_op jit(solution)/shard_map/all_gather | solution.py:17
  16.7 0.7 copy-start.7
  16.7 2.4 copy-start.1
  16.7 92.1 %copy-start.6 = (bf16[2048,128]{1,0:T(8,128)(2,1)S(1)}, bf16[2048,128]{1,0:T(8,128)(2,1)}, u32[]{:S(2)}) copy-start(bf16[2048,128]{1,0:T(8,128)(2,1)} %param.23) | copy-start | bytes 1572868
  20.7 95.3 %copy-start.4 = (f32[128]{0:T(128)S(1)}, f32[128]{0:T(128)}, u32[]{:S(2)}) copy-start(f32[128]{0:T(128)} %param.21) | copy-start | bytes 1540
  20.7 95.3 %copy-start.5 = (f32[128]{0:T(128)S(1)}, f32[128]{0:T(128)}, u32[]{:S(2)}) copy-start(f32[128]{0:T(128)} %param.20) | copy-start | bytes 1540
  154.8 99.2 %copy-start = (bf16[1,64,2048]{2,1,0:T(8,128)(2,1)S(1)}, bf16[1,64,2048]{2,1,0:T(8,128)(2,1)}, u32[]{:S(2)}) copy-start(bf16[1,64,2048]{2,1,0:T(8,128)(2,1)} %param.15) | copy-start | bytes 786436
  154.8 28.8 %all-to-all-start = ((bf16[32,64,128]{2,1,0:T(8,128)(2,1)}), bf16[32,64,128]{2,1,0:T(8,128)(2,1)S(1)}, u32[]{:S(2)}, u32[]{:S(2)}) async-start(bf16[32,64,128]{2,1,0:T(8,128)(2,1)} %bitcast.8), calls=%async_computation | async-start | bytes 1048576 | tf_op jit(solution)/shard_map/all_to_all | solution.py:139
  163.8 99.1 %copy-start.2 = (f32[2048]{0:T(1024)S(1)}, f32[2048]{0:T(1024)}, u32[]{:S(2)}) copy-start(f32[2048]{0:T(1024)} %param.22) | copy-start | bytes 24580
  266.8 110.1 %all-to-all-start.1 = ((bf16[128,6,2048]{2,1,0:T(8,128)(2,1)}), bf16[128,6,2048]{2,1,0:T(8,128)(2,1)}, u32[]{:S(2)}, u32[]{:S(2)}) async-start(bf16[128,6,2048]{2,1,0:T(8,128)(2,1)} %reshape.391), calls=%async_computation.1 | async-start | bytes 8388608 | tf_op jit(solution)/shard_map/all_to_all | solution.py:167
  404.9 8.2 %copy-start.3 = (f32[1,64,8]{1,2,0:T(8,128)S(1)}, f32[1,64,8]{1,2,0:T(8,128)}, u32[]{:S(2)}) copy-start(f32[1,64,8]{1,2,0:T(8,128)} %param.18) | copy-start | bytes 6148
  404.9 104.4 %all-to-all-start.2 = ((bf16[128,6,2048]{2,1,0:T(8,128)(2,1)}), bf16[128,6,2048]{2,1,0:T(8,128)(2,1)}, u32[]{:S(2)}, u32[]{:S(2)}) async-start(bf16[128,6,2048]{2,1,0:T(8,128)(2,1)} %reshape.395), calls=%async_computation.2 | async-start | bytes 8388608 | tf_op jit(solution)/shard_map/all_to_all | solution.py:169
Sparse Core Ops, SparseCore 0:
  9.9 98.8 all-gather.3
  111.4 142.4 all-gather.5
  255.8 27.0 all-gather.7
where the time goes:
time: 530 us; the launch traced here: 529 us
  waiting for transfers between devices  366 us (69%)
  matrix products  48.2 us (9%)
  local copies, waits for them, and re-layouts  42 us (8%)
  starting transfers between devices  28.5 us (5%)
  other arithmetic  22.3 us (4%)
  between operations  13.5 us (3%)
  loops' own time  7.92 us (1%)
    all_to_all x1, waiting for transfers between devices, body(): lax.all_to_all(expert_ffn(flat_rows, full_gate_up, full_down).astype(jnp....  96.1 us
    all_gather x1, waiting for transfers between devices, body(): lax.all_gather(normed, 'seq', axis=0, tiled=True)  88.1 us
    all_to_all x1, waiting for transfers between devices, body(): lax.all_to_all(outgoing, ('grp', 'seq'), split_axis=0, concat_axis=0, til...  88.1 us
    all_gather x1, waiting for transfers between devices, body(): lax.all_gather(w_out, 'seq', axis=0, tiled=True)  70.4 us
    all_to_all x1, waiting for transfers between devices, body(): lax.all_to_all(attended, 'seq', split_axis=0, concat_axis=1, tiled=True)  19.8 us
    all_to_all x1, starting transfers between devices, body(): lax.all_to_all(outgoing, ('grp', 'seq'), split_axis=0, concat_axis=0, til...  13 us
    dot_general x1, matrix products, expert_ffn(): return jnp.dot(hidden, down_proj, preferred_element_type=jnp.float32)  11 us
  transfers between devices with their start and end apart: 6, of which 6 were waited for; matrix products, arithmetic and copies ran while one was open for 13% of the time, Pallas kernels for 0%

commit v1 on v0

--- a/solution.py
+++ b/solution.py
@@ -98,7 +98,9 @@
     keyval_weight = lax.dynamic_index_in_dim(w_keyval, kv_index, 0, keepdims=False)
     joint_weight = jnp.concatenate([w_query, keyval_weight], axis=1)
     projected = jnp.dot(
-        lax.all_gather(normed, "seq", axis=0, tiled=True),
+        jnp.concatenate(
+            lax.all_to_all(jnp.stack([normed] * lax.axis_size("seq")), "seq", 0, 0), axis=0
+        ),
         joint_weight,
         preferred_element_type=jnp.float32,
     ).astype(jnp.bfloat16)

time: 530 us -> 623 us (1.18)
  waiting for transfers between devices: 366 us -> 447 us
  starting transfers between devices: 28.5 us -> 37.1 us
    all_to_all x0 -> x1, waiting for transfers between devices: none -> 246 us  [body(): lax.all_to_all(jnp.stack([normed] * lax.axis_size('seq')), 'seq', 0, 0)]
    all_gather x1 -> x0, waiting for transfers between devices: 88.1 us -> none  [body(): lax.all_gather(normed, 'seq', axis=0, tiled=True)]
    all_gather x1, waiting for transfers between devices: 70.4 us -> 0.01 us  [body(): lax.all_gather(w_out, 'seq', axis=0, tiled=True)]
    all_to_all x0 -> x1, starting transfers between devices: none -> 11.5 us  [body(): lax.all_to_all(jnp.stack([normed] * lax.axis_size('seq')), 'seq', 0, 0)]
  transfers between devices with their start and end apart: 6 -> 6, of which waited for: 6 -> 4; matrix products, arithmetic and copies ran while one was open for 13% -> 12% of each run, Pallas kernels for 0% -> 0%
where the time goes in v1:
time: 623 us; the launch traced here: 622 us
  waiting for transfers between devices  447 us (72%)
  matrix products  48.3 us (8%)
  local copies, waits for them, and re-layouts  45.7 us (7%)
  starting transfers between devices  37.1 us (6%)
  other arithmetic  21.8 us (3%)
  between operations  13.8 us (2%)
  loops' own time  8.47 us (1%)
    all_to_all x1, waiting for transfers between devices, body(): lax.all_to_all(jnp.stack([normed] * lax.axis_size('seq')), 'seq', 0, 0)  246 us
    all_to_all x1, waiting for transfers between devices, body(): lax.all_to_all(expert_ffn(flat_rows, full_gate_up, full_down).astype(jnp....  95.6 us
    all_to_all x1, waiting for transfers between devices, body(): lax.all_to_all(outgoing, ('grp', 'seq'), split_axis=0, concat_axis=0, til...  89.4 us
    all_to_all x1, waiting for transfers between devices, body(): lax.all_to_all(attended, 'seq', split_axis=0, concat_axis=1, tiled=True)  14.6 us
  transfers between devices with their start and end apart: 6, of which 4 were waited for; matrix products, arithmetic and copies ran while one was open for 12% of the time, Pallas kernels for 0%

profile of v1, /device:TPU:32, one launch (start us, length us, event | category | flops | bytes accessed | tf_op | source)
XLA Modules:
  0.0 621.8 jit_solution(9639478033211976096)
XLA Ops:
  6.5 0.7 all-gather.3.cloned.1.call-update
  7.3 1.1 fusion.43
  8.4 1.1 fusion.62
  9.5 4.3 stack.5
  13.8 11.5 %all-to-all-start = ((bf16[32,64,2048]{2,1,0:T(8,128)(2,1)}), bf16[32,64,2048]{2,1,0:T(8,128)(2,1)}, u32[]{:S(2)}, u32[]{:S(2)}) async-start(bf16[32,64,2048]{2,1,0:T(8,128)(2,1)} %stack.5), calls=%async_computation | async-start | bytes 16777216 | tf_op jit(solution)/shard_map/all_to_all | solution.py:102
  25.4 0.9 copy.91
  26.3 4.6 pad_maximum_fusion
  33.6 1.3 dynamic-slice_bitcast_fusion
  34.9 246.2 %all-to-all-done = bf16[32,64,2048]{2,1,0:T(8,128)(2,1)} async-done(((bf16[32,64,2048]{2,1,0:T(8,128)(2,1)}), bf16[32,64,2048]{2,1,0:T(8,128)(2,1)}, u32[]{:S(2)}, u32[]{:S(2)}) %all-to-all-start) | async-done | bytes 8388640 | tf_op jit(solution)/shard_map/all_to_all | solution.py:102
  281.1 6.9 %convolution_convert_fusion.2 = bf16[2048,384]{0,1:T(8,128)(2,1)S(1)} fusion(bf16[2048,2048]{1,0:T(8,128)(2,1)} %bitcast.4, bf16[2048,256]{1,0:T(8,128)(2,1)S(1)} %dynamic-slice_bitcast_fusion, bf16[2048,128]{1,0:T(8,128)(2,1)S(1)} %copy-done.7), kind=kOutput, calls=%fused_computation.27 | convolution fusion | flops 3225157632 | bytes 11534336 | tf_op jit(solution)/shard_map/dot_general | solution.py:100
  288.7 2.4 fusion.51
  291.7 36.4 %while.11 = (s32[]{:T(128)}, bf16[4,512,128]{2,1,0:T(8,128)(2,1)}, s32[4]{0:T(128)S(1)}, f32[2048,64]{0,1:T(8,128)S(1)}, bf16[2048,1,128]{0,2,1:T(8,128)(2,1)S(1...) while((s32[]{:T(128)}, bf16[4,512,128]{2,1,0:T(8,128)(2,1)}, ...), condition=%wide.region_7.8_spmd.clone, body=%wide.region_4.7_spmd.clone.sunk | while | flops 547454464 | bytes 18299552 | solution.py:140
  294.9 1.2 copy.101
  296.1 0.7 iota_add_fusion.2
  296.8 1.8 fusion.112
  298.6 0.7 fusion.113
  299.3 1.5 fusion.114
  304.0 1.2 copy.101
  305.9 1.8 fusion.112
  307.7 0.7 fusion.113
  308.4 1.5 fusion.114
  313.1 1.2 copy.101
  315.0 1.8 fusion.112
  316.8 0.7 fusion.113
  317.5 1.5 fusion.114
  322.2 1.2 copy.101
  323.4 0.7 iota_add_fusion.2
  324.1 1.9 fusion.112
  325.9 0.7 fusion.113
  326.6 1.5 fusion.114
  328.2 8.2 %all-to-all-start.1 = ((bf16[32,64,128]{2,1,0:T(8,128)(2,1)}), bf16[32,64,128]{2,1,0:T(8,128)(2,1)S(1)}, u32[]{:S(2)}, u32[]{:S(2)}) async-start(bf16[32,64,128]{2,1,0:T(8,128)(2,1)} %bitcast.9), calls=%async_computation.1 | async-start | bytes 1048576 | tf_op jit(solution)/shard_map/all_to_all | solution.py:141
  337.8 14.6 %all-to-all-done.1 = bf16[32,64,128]{2,1,0:T(8,128)(2,1)S(1)} async-done(((bf16[32,64,128]{2,1,0:T(8,128)(2,1)}), bf16[32,64,128]{2,1,0:T(8,128)(2,1)S(1)}, u32[]{:S(2)}, u32[]{:S(2)}) %all-to-all-start.1) | async-done | bytes 524320 | tf_op jit(solution)/shard_map/all_to_all | solution.py:141
  352.4 8.8 %fusion.21 = bf16[64,2048]{1,0:T(8,128)(2,1)S(1)} fusion(bf16[4096,2048]{1,0:T(8,128)(2,1)} %all-gather.3.cloned.1.call-done, bf16[1,64,2048]{2,1,0:T(8,128)(2,1)S(1)} %copy-done, bf16[32,64,128]{2,1,0:T(8,128)(2,1)S(1)} %all-to-all-done.1), kind=kOutput, calls=%fused_computation.30 | convolution fusion | flops 1074135040 | bytes 17825792 | tf_op jit(solution)/shard_map/dot_general | solution.py:142
  361.4 1.0 convolution_convert_fusion.1
  362.5 2.9 reshape.409
  365.3 9.2 %all-to-all-start.2 = ((bf16[128,6,2048]{2,1,0:T(8,128)(2,1)}), bf16[128,6,2048]{2,1,0:T(8,128)(2,1)}, u32[]{:S(2)}, u32[]{:S(2)}) async-start(bf16[128,6,2048]{2,1,0:T(8,128)(2,1)} %reshape.409), calls=%async_computation.2 | async-start | bytes 8388608 | tf_op jit(solution)/shard_map/all_to_all | solution.py:169
  374.6 5.8 slice.62
  380.4 89.4 %all-to-all-done.2 = bf16[128,6,2048]{2,1,0:T(8,128)(2,1)} async-done(((bf16[128,6,2048]{2,1,0:T(8,128)(2,1)}), bf16[128,6,2048]{2,1,0:T(8,128)(2,1)}, u32[]{:S(2)}, u32[]{:S(2)}) %all-to-all-start.2) | async-done | bytes 3145760 | tf_op jit(solution)/shard_map/all_to_all | solution.py:169
  469.9 4.9 reshape.410
  474.7 5.9 fusion.20
  480.6 11.0 %convolution_convert_fusion = bf16[768,2048]{1,0:T(8,128)(2,1)} fusion(bf16[768,6144]{0,1:T(8,128)(2,1)} %all-gather.5.cloned.1.call-done, f32[768,768]{1,0:T(8,128)} %fusion.20, bf16[768,2048]{1,0:T(8,128)(2,1)S(1)} %reshape.410, bf16[2,2048,768]{2,1,0:T(8,128)(2,1)} %bitcast.142), kind=kOutput, calls=%fused_computation.20 | convolution fusion | flops 4836950016 | bytes 14942208 | tf_op jit(solution)/shard_map/dot_general | solution.py:67
  491.6 6.3 %reshape.413 = bf16[128,6,2048]{2,1,0:T(8,128)(2,1)} reshape(bf16[768,2048]{1,0:T(8,128)(2,1)} %convolution_convert_fusion) | data formatting | bytes 6291456 | tf_op jit(solution)/shard_map/reshape | solution.py:172
  497.9 8.1 %all-to-all-start.3 = ((bf16[128,6,2048]{2,1,0:T(8,128)(2,1)}), bf16[128,6,2048]{2,1,0:T(8,128)(2,1)}, u32[]{:S(2)}, u32[]{:S(2)}) async-start(bf16[128,6,2048]{2,1,0:T(8,128)(2,1)} %reshape.413), calls=%async_computation.3 | async-start | bytes 8388608 | tf_op jit(solution)/shard_map/all_to_all | solution.py:171
  506.4 95.6 %all-to-all-done.3 = bf16[128,6,2048]{2,1,0:T(8,128)(2,1)} async-done(((bf16[128,6,2048]{2,1,0:T(8,128)(2,1)}), bf16[128,6,2048]{2,1,0:T(8,128)(2,1)}, u32[]{:S(2)}, u32[]{:S(2)}) %all-to-all-start.3) | async-done | bytes 3145760 | tf_op jit(solution)/shard_map/all_to_all | solution.py:171
  602.0 4.9 reshape.414
  606.8 3.3 gather_fusion
  610.2 4.0 multiply_reduce_fusion
  614.2 0.8 fusion.60
  (88 shorter events, 11.4 us)
Async XLA Ops:
  6.5 345.9 %all-gather.3.cloned.1.call-start = ((), (), s32[]{:S(2)}) async-start(), calls=%async_computation.4 | async-start | bytes 17301504 | tf_op jit(solution)/shard_map/all_gather | solution.py:144
  13.8 11.6 %copy-start.1 = (bf16[1,384,2048]{2,1,0:T(8,128)(2,1)S(1)}, bf16[1,384,2048]{2,1,0:T(8,128)(2,1)}, u32[]{:S(2)}) copy-start(bf16[1,384,2048]{2,1,0:T(8,128)(2,1)} %param.27) | copy-start | bytes 4718596
  13.8 267.3 %all-to-all-start = ((bf16[32,64,2048]{2,1,0:T(8,128)(2,1)}), bf16[32,64,2048]{2,1,0:T(8,128)(2,1)}, u32[]{:S(2)}, u32[]{:S(2)}) async-start(bf16[32,64,2048]{2,1,0:T(8,128)(2,1)} %stack.5), calls=%async_computation | async-start | bytes 16777216 | tf_op jit(solution)/shard_map/all_to_all | solution.py:102
  25.4 349.2 %all-gather.5.cloned.1.call-start = ((), (), s32[]{:S(2)}) async-start(), calls=%async_computation.5 | async-start | bytes 14155776 | tf_op jit(solution)/shard_map/all_gather | solution.py:17
  30.9 0.7 copy-start.8
  30.9 2.4 copy-start.2
  30.9 250.2 %copy-start.7 = (bf16[2048,128]{1,0:T(8,128)(2,1)S(1)}, bf16[2048,128]{1,0:T(8,128)(2,1)}, u32[]{:S(2)}) copy-start(bf16[2048,128]{1,0:T(8,128)(2,1)} %param.23) | copy-start | bytes 1572868
  281.1 7.3 %copy-start.5 = (f32[128]{0:T(128)S(1)}, f32[128]{0:T(128)}, u32[]{:S(2)}) copy-start(f32[128]{0:T(128)} %param.21) | copy-start | bytes 1540
  281.1 7.3 %copy-start.6 = (f32[128]{0:T(128)S(1)}, f32[128]{0:T(128)}, u32[]{:S(2)}) copy-start(f32[128]{0:T(128)} %param.20) | copy-start | bytes 1540
  328.2 24.3 %copy-start = (bf16[1,64,2048]{2,1,0:T(8,128)(2,1)S(1)}, bf16[1,64,2048]{2,1,0:T(8,128)(2,1)}, u32[]{:S(2)}) copy-start(bf16[1,64,2048]{2,1,0:T(8,128)(2,1)} %param.15) | copy-start | bytes 786436
  328.2 24.3 %all-to-all-start.1 = ((bf16[32,64,128]{2,1,0:T(8,128)(2,1)}), bf16[32,64,128]{2,1,0:T(8,128)(2,1)S(1)}, u32[]{:S(2)}, u32[]{:S(2)}) async-start(bf16[32,64,128]{2,1,0:T(8,128)(2,1)} %bitcast.9), calls=%async_computation.1 | async-start | bytes 1048576 | tf_op jit(solution)/shard_map/all_to_all | solution.py:141
  337.8 23.6 %copy-start.3 = (f32[2048]{0:T(1024)S(1)}, f32[2048]{0:T(1024)}, u32[]{:S(2)}) copy-start(f32[2048]{0:T(1024)} %param.22) | copy-start | bytes 24580
  365.3 104.5 %all-to-all-start.2 = ((bf16[128,6,2048]{2,1,0:T(8,128)(2,1)}), bf16[128,6,2048]{2,1,0:T(8,128)(2,1)}, u32[]{:S(2)}, u32[]{:S(2)}) async-start(bf16[128,6,2048]{2,1,0:T(8,128)(2,1)} %reshape.409), calls=%async_computation.2 | async-start | bytes 8388608 | tf_op jit(solution)/shard_map/all_to_all | solution.py:169
  497.9 8.4 %copy-start.4 = (f32[1,64,8]{1,2,0:T(8,128)S(1)}, f32[1,64,8]{1,2,0:T(8,128)}, u32[]{:S(2)}) copy-start(f32[1,64,8]{1,2,0:T(8,128)} %param.18) | copy-start | bytes 6148
  497.9 104.1 %all-to-all-start.3 = ((bf16[128,6,2048]{2,1,0:T(8,128)(2,1)}), bf16[128,6,2048]{2,1,0:T(8,128)(2,1)}, u32[]{:S(2)}, u32[]{:S(2)}) async-start(bf16[128,6,2048]{2,1,0:T(8,128)(2,1)} %reshape.413), calls=%async_computation.3 | async-start | bytes 8388608 | tf_op jit(solution)/shard_map/all_to_all | solution.py:171
Sparse Core Ops, SparseCore 0:
  9.9 296.3 all-gather.2
  308.1 26.9 all-gather.4
